TPU v7x, 256 devices: a whole 4x4x8 slice. The times are simulated.
256 devices in a mesh: region: 8 (over x, core), sub: 32 (over y, z).
Axes of the slice: x: 4, y: 4, z: 8, core: 2. Of those that a mesh axis runs over, the one named last changes fastest.
Arguments:
- multipliers: float32 [256, 3, 3, 256], P(('region', 'sub')), may hold values from -6 to 6
- direction: float32 [256, 3, 3, 256], P(('region', 'sub')), may hold values from -12 to 12
- residual: float32 [256, 3, 3, 256], P(('region', 'sub')), may hold values from -12 to 12
- reaction: float32 [256, 16, 256], P(('region', 'sub')), may hold values from 0.1 to 2
- viscosity: float32 [256, 16, 256], P(('region', 'sub')), may hold values from 0.5 to 5
- primal_index: int32 [256, 96], P(('region', 'sub')), may hold values from 17 to 2286, as said below
- region_inverse: float32 [8, 3072, 3072], P('region', 'sub'), as said below
- coarse_map: float32 [256, 96, 384], P(('region', 'sub')), may hold values from -0.4375 to 0.4375
- global_inverse: float32 [384, 384], replicated, as said below
Outputs:
- new_multipliers: float32 [256, 3, 3, 256], P(('region', 'sub'))
- new_residual: float32 [256, 3, 3, 256], P(('region', 'sub'))
- velocity: float32 [256, 3, 16, 256], P(('region', 'sub'))
- pressure: float32 [256, 16, 256], P(('region', 'sub'))
Inputs may be any that keep to these rules, and one draw needn't show every extreme that they name: `primal_index`: each row holds 96 different positions, each in the interior of a face (neither face index 0 nor 16 - 1); every row contains the first such position and the last one. `region_inverse`: each region's matrix is symmetric positive definite. `global_inverse`: symmetric positive definite.
All inputs are finite; a program needn't handle non-finite values.
Results may differ from a plain program's by a relative error of at most 0.0001.
Values sent between devices are 32-bit elements; how exact they have to be, the bound alone decides.
A program may use at most 64 MiB of HBM per device.

v0:
```python
import jax
import jax.numpy as jnp
from jax import lax
from jax.sharding import PartitionSpec as P

DOM_Z = 4
LEVELS = 3
SWEEPS = 1
COARSE_SWEEPS = 8
VCYCLES = 2
damping = 0.8


def shifted_2(x, axis, by):
    count = lax.axis_size(axis)
    return lax.ppermute(x, axis, [(i, (i + by) % count) for i in range(count)])


def operate(field, react, weight, cells):
    width = field.shape[-1]
    padded = jnp.pad(field, ((0, 0), (1, 1), (cells, cells)))
    middle = padded[:, 1:-1]
    position = lax.broadcasted_iota(jnp.int32, (1, 1, width), 2) % cells
    above = jnp.where(position < cells - 1, middle[:, :, cells + 1 : cells + 1 + width], 0.0)
    beneath = jnp.where(position > 0, middle[:, :, cells - 1 : cells - 1 + width], 0.0)
    beside = padded[:, 2:, cells : cells + width] + padded[:, :-2, cells : cells + width]
    beside = beside + middle[:, :, 2 * cells :] + middle[:, :, :width]
    beside = beside + above + beneath
    return react * field + weight * (6.0 * field - beside)


def restrict(array, cells):
    lead = array.shape[:-2]
    depth = array.shape[-2]
    half = cells // 2
    blocks = array.reshape(lead + (depth // 2, 2, half, 2, half, 2)).mean(axis=(-5, -3, -1))
    return blocks.reshape(lead + (depth // 2, half * half))


def prolong(array, cells):
    lead = array.shape[:-2]
    depth = array.shape[-2]
    cubic = array.reshape(lead + (depth, cells, cells))
    grown = jnp.repeat(jnp.repeat(jnp.repeat(cubic, 2, axis=-3), 2, axis=-2), 2, axis=-1)
    return grown.reshape(lead + (2 * depth, 4 * cells * cells))


def relax(field, source, react, weight, cells, count):
    diagonal = react + 6.0 * weight
    for _ in range(count):
        field = field + damping * (source - operate(field, react, weight, cells)) / diagonal
    return field


def vcycle(field, source, reacts, cells, level):
    weight = 0.25**level
    if level == LEVELS - 1:
        return relax(field, source, reacts[level], weight, cells, COARSE_SWEEPS)
    field = relax(field, source, reacts[level], weight, cells, SWEEPS)
    remain = restrict(source - operate(field, reacts[level], weight, cells), cells)
    coarse = vcycle(jnp.zeros_like(remain), remain, reacts, cells // 2, level + 1)
    field = field + prolong(coarse, cells // 2)
    return relax(field, source, reacts[level], weight, cells, SWEEPS)


def local_solve(source, react, cells):
    reacts = [react]
    size_now = cells
    for _ in range(LEVELS - 1):
        reacts.append(restrict(reacts[-1], size_now))
        size_now = size_now // 2
    field = jnp.zeros_like(source)
    for _ in range(VCYCLES):
        field = vcycle(field, source, reacts, cells, 0)
    return field


def face_cells(picked, cells):
    face = cells * cells
    block = picked // (3 * face)
    component = picked // face % 3
    spot = picked % face
    first = spot // cells
    second = spot % cells
    upper = cells - 1
    place = jnp.where(
        block == 0,
        upper * face + spot,
        jnp.where(
            block == 1, first * face + upper * cells + second, first * face + second * cells + upper
        ),
    )
    return component * (cells * face) + place


def body(
    multipliers,
    direction,
    residual,
    reaction,
    viscosity,
    primal_index,
    region_inverse,
    coarse_map,
    global_inverse,
):
    highest = lax.Precision.HIGHEST
    react = reaction[0]
    cells = react.shape[0]
    face = react.shape[1]
    upper_end = cells - 1
    active = direction[0]
    below_x = shifted_2(active[0], "region", 1)
    below_y = shifted_2(active[1], "sub", DOM_Z)
    below_z = shifted_2(active[2], "sub", 1)
    source = jnp.zeros((3, cells, face), jnp.float32)
    source = source.at[:, upper_end, :].add(active[0])
    source = source.at[:, :, face - cells :].add(active[1].reshape(3, cells, cells))
    source = source.at[:, :, upper_end::cells].add(active[2].reshape(3, cells, cells))
    source = source.at[:, 0, :].add(-below_x)
    source = source.at[:, :, :cells].add(-below_y.reshape(3, cells, cells))
    source = source.at[:, :, 0::cells].add(-below_z.reshape(3, cells, cells))
    picked = primal_index[0]
    primal = jnp.take(active.reshape(-1), picked)
    rows = region_inverse[0]
    mapping = coarse_map[0]
    share = jnp.dot(primal, mapping, precision=highest)
    total = lax.psum(share, ("region", "sub"))
    region_part = jnp.dot(
        rows, lax.all_gather(primal, "sub", axis=0, tiled=True), precision=highest
    )
    top = jnp.dot(global_inverse, total, precision=highest)
    lifted = region_part + jnp.dot(mapping, top, precision=highest)
    base = local_solve(source, react, cells)
    spots = face_cells(picked, cells)
    velocity = base.reshape(-1).at[spots].add(lifted).reshape(3, cells, face)
    upper_x = velocity[:, upper_end, :]
    upper_y = velocity[:, :, face - cells :].reshape(3, face)
    upper_z = velocity[:, :, upper_end::cells].reshape(3, face)
    lower_x = velocity[:, 0, :]
    lower_y = velocity[:, :, :cells].reshape(3, face)
    lower_z = velocity[:, :, 0::cells].reshape(3, face)
    squares = jnp.sum(residual[0] * residual[0])
    after_x = shifted_2(lower_x, "region", -1)
    after_y = shifted_2(lower_y, "sub", -DOM_Z)
    after_z = shifted_2(lower_z, "sub", -1)
    jump = jnp.stack([upper_x - after_x, upper_y - after_y, upper_z - after_z])
    curvature, squares_all = lax.psum((jnp.sum(active * jump), squares), ("region", "sub"))
    step_x = jnp.concatenate([velocity[0, 1:], after_x[0][None]], axis=0) - velocity[0]
    step_y = (
        jnp.concatenate([velocity[1][:, cells:], after_y[1].reshape(cells, cells)], axis=1)
        - velocity[1]
    )
    position = lax.broadcasted_iota(jnp.int32, (1, face), 1) % cells
    edge_values = jnp.repeat(after_z[2].reshape(cells, cells), cells, axis=1)
    shifted = jnp.pad(velocity[2][:, 1:], ((0, 0), (0, 1)))
    step_z = jnp.where(position == cells - 1, edge_values, shifted) - velocity[2]
    pressure = -viscosity[0] * (step_x + step_y + step_z)
    alpha = squares_all / curvature
    new_multipliers = (multipliers[0] + alpha * active)[None]
    new_residual = (residual[0] - alpha * jump)[None]
    return (new_multipliers, new_residual, velocity[None], pressure[None])


def solution(mesh):
    in_specs = (
        P(("region", "sub"), None, None, None),
        P(("region", "sub"), None, None, None),
        P(("region", "sub"), None, None, None),
        P(("region", "sub"), None, None),
        P(("region", "sub"), None, None),
        P(("region", "sub"), None),
        P("region", "sub", None),
        P(("region", "sub"), None, None),
        P(),
    )
    out_specs = (
        P(("region", "sub"), None, None, None),
        P(("region", "sub"), None, None, None),
        P(("region", "sub"), None, None, None),
        P(("region", "sub"), None, None),
    )
    return jax.shard_map(body, mesh=mesh, in_specs=in_specs, out_specs=out_specs, check_vma=False)
```

profile of v0, /device:TPU:1, one launch (start us, length us, event | category | flops | bytes accessed | tf_op | source)
XLA Modules:
  0.0 369.7 jit_solution(10086883032054162801)
XLA Ops:
  0.6 0.8 fusion.286
  1.5 2.6 collective-permute-start
  4.1 6.9 %collective-permute-start.1 = (f32[3,256]{1,0:T(4,128)S(1)}, f32[3,256]{1,0:T(4,128)S(1)}, u32[]{:S(2)}, u32[]{:S(2)}) collective-permute-start(f32[3,256]{1,0:T(4,128)S(1)} %bitcast.181), channel_id=1, source_target_pairs={{0,4},{1,5},{2,6},{3,7},{4,8},{5,9},{6,10},{7,11},{8,12},{9,13},{1... | collective-permute-start | bytes 9224 | tf_op jit(solution)/shard_map/ppermute | solution.py:16
  11.0 0.7 collective-permute-start.2
  11.8 0.7 add_bitcast_fusion
  12.5 0.7 broadcast_multiply_fusion.6
  13.2 1.7 reshape_squeeze.17
  15.4 0.3 copy.126
  15.7 0.3 scatter-add.34
  16.5 1.1 gather_fusion
  17.7 0.6 dynamic-slice.29
  19.1 114.8 %all-reduce.28 = f32[3072]{0:T(1024)S(1)} all-reduce(f32[3072]{0:T(1024)S(1)} %fusion.269), channel_id=1, replica_groups=mesh['region'=8,'sub'=32] {'sub'}, use_global_device_ids=true, to_apply=%add.28 | all-reduce | flops 3072 | bytes 24576
  133.8 0.2 convolution_reduce_fusion
  134.0 100.0 %psum.22 = f32[384]{0:T(512)S(1)} all-reduce(f32[384]{0:T(512)S(1)} %convolution_reduce_fusion), channel_id=1, replica_groups=mesh['region'=8,'sub'=32] {'region','sub'}, use_global_device_ids=true, to_apply=%region_10.11 | all-reduce | flops 384 | bytes 3072 | tf_op jit(solution)/shard_map/psum | solution.py:128
  234.1 0.6 multiply_reduce_fusion
  234.7 1.0 fusion.2
  235.7 0.6 convolution_bitcast_fusion
  236.3 0.3 fusion.5
  237.5 1.1 scatter_fusion
  238.6 0.3 copy.129
  239.4 4.3 %scatter-add.44 = f32[3,16,256]{1,0,2:T(4,128)S(1)} dynamic-update-slice(f32[3,16,256]{1,0,2:T(4,128)S(1)} %scatter_fusion, f32[3,1,256]{1,0,2:T(4,128)S(1)} %slice_add_fusion, s32[]{:T(128)} %constant.334.clone.1, s32[]{:T(128)} %constant.334.clone.1, s32[]{:T(128)} %constant.334.clone.1) | dynamic-update-slice | bytes 6148 | tf_op jit(solution)/shard_map/scatter-add | solution.py:120
  243.7 1.1 scatter_fusion.1
  244.8 2.0 fusion.17
  246.9 2.0 add_subtract_fusion.1
  249.0 4.8 %reshape.713 = f32[3,8,2,8,2,8,2]{6,5,4,3,2,1,0:T(8,128)} reshape(f32[3,16,256]{2,1,0:T(8,128)S(1)} %copy.135) | data formatting | bytes 98304 | tf_op jit(solution)/shard_map/reshape | solution.py:36
  253.8 2.2 reduce_sum.73
  256.6 0.5 reshape.714
  257.1 0.2 reduce_sum.75
  259.1 2.1 bitcast_add_fusion.1
  261.2 2.1 divide_add_fusion.2
  263.3 2.1 divide_add_fusion.1
  265.3 2.2 add_subtract_fusion
  267.7 4.8 %reshape.721 = f32[3,8,2,8,2,8,2]{6,5,4,3,2,1,0:T(8,128)} reshape(f32[3,16,256]{2,1,0:T(8,128)S(1)} %copy.147) | data formatting | bytes 98304 | tf_op jit(solution)/shard_map/reshape | solution.py:36
  272.5 2.2 reduce_sum.77
  275.2 0.5 reshape.722
  275.7 0.2 reduce_sum.78
  277.9 2.1 divide_add_fusion
  280.2 1.1 scatter_fusion.2
  281.4 1.1 collective-permute-start.3
  282.9 0.6 broadcast_in_dim_reshape.2
  283.6 1.3 collective-permute-start.5
  285.0 2.1 collective-permute-start.4
  287.8 3.6 collective-permute-done.4
  291.4 0.6 fusion.100
  292.1 74.3 %all-reduce.29 = (f32[]{:T(128)}, f32[]{:T(128)}) all-reduce(f32[]{:T(128)} %multiply_reduce_fusion, f32[]{:T(128)} %fusion.100), channel_id=1, replica_groups=mesh['region'=8,'sub'=32] {'region','sub'}, use_global_device_ids=true, to_apply=%region_1.0 | all-reduce | flops 2 | bytes 16 | tf_op jit(solution)/shard_map/psum | solution.py:148
  367.8 0.6 copy.163
  368.4 0.6 copy.162
  369.0 0.7 fusion.99
  (162 shorter events, 8.9 us)
Async XLA Ops:
  0.6 234.1 %copy-start = (f32[1,96,3072]{2,1,0:T(8,128)S(1)}, f32[1,96,3072]{2,1,0:T(8,128)}, u32[]{:S(2)}) copy-start(f32[1,96,3072]{2,1,0:T(8,128)} %param.23) | copy-start | bytes 3538948
  1.5 237.1 %collective-permute-start = (f32[3,256]{1,0:T(4,128)S(1)}, f32[3,256]{1,0:T(4,128)S(1)}, u32[]{:S(2)}, u32[]{:S(2)}) collective-permute-start(f32[3,256]{1,0:T(4,128)S(1)} %bitcast.182), channel_id=1, source_target_pairs={{0,32},{32,64},{64,96},{96,128},{128,160},{160,192},{192,224},{224... | collective-permute-start | bytes 9224 | tf_op jit(solution)/shard_map/ppermute | solution.py:16
  4.1 234.8 %collective-permute-start.1 = (f32[3,256]{1,0:T(4,128)S(1)}, f32[3,256]{1,0:T(4,128)S(1)}, u32[]{:S(2)}, u32[]{:S(2)}) collective-permute-start(f32[3,256]{1,0:T(4,128)S(1)} %bitcast.181), channel_id=1, source_target_pairs={{0,4},{1,5},{2,6},{3,7},{4,8},{5,9},{6,10},{7,11},{8,12},{9,13},{1... | collective-permute-start | bytes 9224 | tf_op jit(solution)/shard_map/ppermute | solution.py:16
  11.0 228.0 %collective-permute-start.2 = (f32[3,256]{1,0:T(4,128)S(1)}, f32[3,256]{1,0:T(4,128)S(1)}, u32[]{:S(2)}, u32[]{:S(2)}) collective-permute-start(f32[3,256]{1,0:T(4,128)S(1)} %bitcast.180), channel_id=1, source_target_pairs={{0,1},{1,2},{2,3},{3,4},{4,5},{5,6},{6,7},{7,8},{8,9},{9,10},{10,1... | collective-permute-start | bytes 9224 | tf_op jit(solution)/shard_map/ppermute | solution.py:16
  15.1 1.3 copy-start.8
  15.1 1.3 copy-start.4
  15.4 2.3 copy-start.9
  15.4 118.4 %copy-start.2 = (f32[1,96,384]{2,1,0:T(8,128)S(1)}, f32[1,96,384]{2,1,0:T(8,128)}, u32[]{:S(2)}) copy-start(f32[1,96,384]{2,1,0:T(8,128)} %param.24) | copy-start | bytes 442372
  15.6 218.4 %copy-start.5 = (f32[1,3,3,256]{3,0,2,1:T(1,128)S(1)}, f32[1,3,3,256]{3,0,2,1:T(1,128)}, u32[]{:S(2)}) copy-start(f32[1,3,3,256]{3,0,2,1:T(1,128)} %param.19) | copy-start | bytes 27652
  16.0 219.7 %copy-start.1 = (f32[384,384]{1,0:T(8,128)S(1)}, f32[384,384]{1,0:T(8,128)}, u32[]{:S(2)}) copy-start(f32[384,384]{1,0:T(8,128)} %param.25) | copy-start | bytes 1769476
  234.7 2.4 copy-start.3
  280.2 88.2 %copy-start.7 = (f32[1,3,3,256]{3,0,2,1:T(1,128)S(1)}, f32[1,3,3,256]{3,0,2,1:T(1,128)}, u32[]{:S(2)}) copy-start(f32[1,3,3,256]{3,0,2,1:T(1,128)} %param.17) | copy-start | bytes 27652
  280.2 88.8 %copy-start.6 = (f32[1,16,256]{2,1,0:T(8,128)S(1)}, f32[1,16,256]{2,1,0:T(8,128)}, u32[]{:S(2)}) copy-start(f32[1,16,256]{2,1,0:T(8,128)} %param.21) | copy-start | bytes 49156
  281.4 6.0 %collective-permute-start.3 = (f32[3,256]{1,0:T(4,128)S(1)}, f32[3,256]{1,0:T(4,128)S(1)}, u32[]{:S(2)}, u32[]{:S(2)}) collective-permute-start(f32[3,256]{1,0:T(4,128)S(1)} %bitcast.183), channel_id=1, source_target_pairs={{0,224},{32,0},{64,32},{96,64},{128,96},{160,128},{192,160},{224,1... | collective-permute-start | bytes 9224 | tf_op jit(solution)/shard_map/ppermute | solution.py:16
  283.6 3.8 %collective-permute-start.5 = (f32[3,256]{1,0:T(4,128)S(1)}, f32[3,256]{1,0:T(4,128)S(1)}, u32[]{:S(2)}, u32[]{:S(2)}) collective-permute-start(f32[3,256]{1,0:T(4,128)S(1)} %reshape.734), channel_id=1, source_target_pairs={{0,31},{1,0},{2,1},{3,2},{4,3},{5,4},{6,5},{7,6},{8,7},{9,8},{10,9... | collective-permute-start | bytes 9224 | tf_op jit(solution)/shard_map/ppermute | solution.py:16
  285.0 6.4 %collective-permute-start.4 = (f32[3,256]{1,0:T(4,128)S(1)}, f32[3,256]{1,0:T(4,128)S(1)}, u32[]{:S(2)}, u32[]{:S(2)}) collective-permute-start(f32[3,256]{1,0:T(4,128)S(1)} %reshape.732), channel_id=1, source_target_pairs={{0,28},{1,29},{2,30},{3,31},{4,0},{5,1},{6,2},{7,3},{8,4},{9,5},{1... | collective-permute-start | bytes 9224 | tf_op jit(solution)/shard_map/ppermute | solution.py:16
where the time goes:
time: 371 us; the launch traced here: 370 us
  blocking collectives  289 us (78%)
  other arithmetic  29.4 us (8%)
  local copies, waits for them, and re-layouts  27.2 us (7%)
  starting transfers between devices  14.8 us (4%)
    unnamed x1, blocking collectives  115 us
    psum x1, blocking collectives, body(): total = lax.psum(share, ('region', 'sub'))  100 us
    psum x1, blocking collectives, body(): lax.psum((jnp.sum(active * jump), squares), ('region', 'sub'))  74.3 us
    ppermute x6, starting transfers between devices, shifted_2(): return lax.ppermute(x, axis, [(i, (i + by) % count) for i in range(count)])  14.8 us
    reshape x4, local copies, waits for them, and re-layouts, restrict(): array.reshape(lead + (depth // 2, 2, half, 2, half, 2))  10.7 us
    add x17, other arithmetic, relax(): field + damping * (source - operate(field, react, weight, cells)) / diagonal  7.44 us
  transfers between devices with their start and end apart: 6, of which 1 were waited for; matrix products, arithmetic and copies ran while one was open for 4% of the time, Pallas kernels for 0%

commit v1 on v0

--- a/solution.py
+++ b/solution.py
@@ -1,3 +1,4 @@
+import functools
 import jax
 import jax.numpy as jnp
 from jax import lax
@@ -9,6 +10,15 @@
 COARSE_SWEEPS = 8
 VCYCLES = 2
 damping = 0.8
+
+
+def track_frame_for(local_x, which_axis, bus_axis):
+    for u in (which_axis, bus_axis):
+        local_x = lax.psum(local_x, axis_name=u)
+    return local_x
+
+
+number_target = functools.partial(track_frame_for, which_axis="sub", bus_axis="region")
 
 
 def shifted_2(x, axis, by):
@@ -125,7 +135,7 @@
     rows = region_inverse[0]
     mapping = coarse_map[0]
     share = jnp.dot(primal, mapping, precision=highest)
-    total = lax.psum(share, ("region", "sub"))
+    total = number_target(share)
     region_part = jnp.dot(
         rows, lax.all_gather(primal, "sub", axis=0, tiled=True), precision=highest
     )

time: 371 us -> 307 us (0.83)
  blocking collectives: 289 us -> 227 us
  starting transfers between devices: 14.8 us -> 11 us
    psum x1, blocking collectives: 100 us -> 38.7 us  [track_frame_for(): local_x = lax.psum(local_x, axis_name=u)]
    ppermute x6, starting transfers between devices: 14.8 us -> 11 us  [shifted_2(): return lax.ppermute(x, axis, [(i, (i + by) % count) for i in range(count)])]
  transfers between devices with their start and end apart: 6 -> 6, of which waited for: 1 -> 3; matrix products, arithmetic and copies ran while one was open for 4% -> 4% of each run, Pallas kernels for 0% -> 0%
where the time goes in v1:
time: 307 us; the launch traced here: 306 us
  blocking collectives  227 us (74%)
  other arithmetic  29.4 us (10%)
  local copies, waits for them, and re-layouts  27.2 us (9%)
  starting transfers between devices  11 us (4%)
  waiting for transfers between devices  5.69 us (2%)
  between operations  3.48 us (1%)
    unnamed x1, blocking collectives  115 us
    psum x1, blocking collectives, body(): lax.psum((jnp.sum(active * jump), squares), ('region', 'sub'))  74 us
    psum x1, blocking collectives, track_frame_for(): local_x = lax.psum(local_x, axis_name=u)  38.7 us
    ppermute x6, starting transfers between devices, shifted_2(): return lax.ppermute(x, axis, [(i, (i + by) % count) for i in range(count)])  11 us
    reshape x4, local copies, waits for them, and re-layouts, restrict(): array.reshape(lead + (depth // 2, 2, half, 2, half, 2))  10.7 us
    add x17, other arithmetic, relax(): field + damping * (source - operate(field, react, weight, cells)) / diagonal  7.44 us
  transfers between devices with their start and end apart: 6, of which 3 were waited for; matrix products, arithmetic and copies ran while one was open for 4% of the time, Pallas kernels for 0%

profile of v1, /device:TPU:1, one launch (start us, length us, event | category | flops | bytes accessed | tf_op | source)
XLA Modules:
  0.0 306.3 jit_solution(13002154702716550348)
XLA Ops:
  0.6 0.8 fusion.286
  1.5 2.6 collective-permute-start
  4.1 6.9 %collective-permute-start.1 = (f32[3,256]{1,0:T(4,128)S(1)}, f32[3,256]{1,0:T(4,128)S(1)}, u32[]{:S(2)}, u32[]{:S(2)}) collective-permute-start(f32[3,256]{1,0:T(4,128)S(1)} %bitcast.181), channel_id=1, source_target_pairs={{0,4},{1,5},{2,6},{3,7},{4,8},{5,9},{6,10},{7,11},{8,12},{9,13},{1... | collective-permute-start | bytes 9224 | tf_op jit(solution)/shard_map/ppermute | solution.py:26
  11.0 0.7 collective-permute-start.2
  11.8 0.7 add_bitcast_fusion
  12.5 0.7 broadcast_multiply_fusion.6
  13.2 1.7 reshape_squeeze.17
  15.4 0.3 copy.126
  15.7 0.3 scatter-add.34
  16.5 1.1 gather_fusion
  17.7 0.6 dynamic-slice.29
  18.9 0.2 convolution_reduce_fusion
  19.3 114.8 %all-reduce.30 = (f32[3072]{0:T(1024)S(1)}, f32[384]{0:T(512)S(1)}) all-reduce(f32[3072]{0:T(1024)S(1)} %fusion.269, f32[384]{0:T(512)S(1)} %convolution_reduce_fusion), channel_id=1, replica_groups=mesh['region'=8,'sub'=32] {'sub'}, use_global_device_ids=true, to_apply=%add.28 | all-reduce | flops 3456 | bytes 27648
  134.0 38.7 %psum.30 = f32[384]{0:T(512)S(1)} all-reduce(f32[384]{0:T(512)S(1)} %get-tuple-element.77), channel_id=1, replica_groups=mesh['region'=8,'sub'=32] {'region'}, use_global_device_ids=true, to_apply=%region_11.12 | all-reduce | flops 384 | bytes 3072 | tf_op jit(solution)/shard_map/psum | solution.py:17
  172.8 0.6 multiply_reduce_fusion
  173.4 0.6 convolution_bitcast_fusion
  174.0 1.1 fusion.2
  175.1 0.2 fusion.5
  176.2 1.1 scatter_fusion
  177.3 0.3 copy.129
  178.1 4.3 %scatter-add.44 = f32[3,16,256]{1,0,2:T(4,128)S(1)} dynamic-update-slice(f32[3,16,256]{1,0,2:T(4,128)S(1)} %scatter_fusion, f32[3,1,256]{1,0,2:T(4,128)S(1)} %slice_add_fusion, s32[]{:T(128)} %constant.334.clone.1, s32[]{:T(128)} %constant.334.clone.1, s32[]{:T(128)} %constant.334.clone.1) | dynamic-update-slice | bytes 6148 | tf_op jit(solution)/shard_map/scatter-add | solution.py:130
  182.4 1.1 scatter_fusion.1
  183.6 2.0 fusion.17
  185.6 2.0 add_subtract_fusion.1
  187.7 4.8 %reshape.713 = f32[3,8,2,8,2,8,2]{6,5,4,3,2,1,0:T(8,128)} reshape(f32[3,16,256]{2,1,0:T(8,128)S(1)} %copy.135) | data formatting | bytes 98304 | tf_op jit(solution)/shard_map/reshape | solution.py:46
  192.6 2.2 reduce_sum.73
  195.3 0.5 reshape.714
  195.8 0.2 reduce_sum.75
  197.9 2.1 bitcast_add_fusion.1
  199.9 2.1 divide_add_fusion.2
  202.0 2.1 divide_add_fusion.1
  204.1 2.2 add_subtract_fusion
  206.4 4.8 %reshape.721 = f32[3,8,2,8,2,8,2]{6,5,4,3,2,1,0:T(8,128)} reshape(f32[3,16,256]{2,1,0:T(8,128)S(1)} %copy.147) | data formatting | bytes 98304 | tf_op jit(solution)/shard_map/reshape | solution.py:46
  211.3 2.2 reduce_sum.77
  214.0 0.5 reshape.722
  214.5 0.2 reduce_sum.78
  216.6 2.1 divide_add_fusion
  218.9 1.1 scatter_fusion.2
  220.2 0.7 collective-permute-start.3
  221.2 0.6 broadcast_in_dim_reshape.2
  222.4 0.8 collective-permute-done.3
  223.2 1.2 collective-permute-done.5
  224.7 3.7 %collective-permute-done.4 = f32[3,256]{1,0:T(4,128)S(1)} collective-permute-done((f32[3,256]{1,0:T(4,128)S(1)}, f32[3,256]{1,0:T(4,128)S(1)}, u32[]{:S(2)}, u32[]{:S(2)}) %collective-permute-start.4) | collective-permute-done | bytes 3104 | tf_op jit(solution)/shard_map/ppermute | solution.py:26
  228.4 0.6 fusion.100
  229.1 74.0 %all-reduce.29 = (f32[]{:T(128)}, f32[]{:T(128)}) all-reduce(f32[]{:T(128)} %multiply_reduce_fusion, f32[]{:T(128)} %fusion.100), channel_id=1, replica_groups=mesh['region'=8,'sub'=32] {'region','sub'}, use_global_device_ids=true, to_apply=%region_1.0 | all-reduce | flops 2 | bytes 16 | tf_op jit(solution)/shard_map/psum | solution.py:158
  304.4 0.6 copy.163
  305.0 0.6 copy.162
  305.6 0.7 fusion.99
  (162 shorter events, 8.9 us)
Async XLA Ops:
  0.6 173.4 %copy-start = (f32[1,96,3072]{2,1,0:T(8,128)S(1)}, f32[1,96,3072]{2,1,0:T(8,128)}, u32[]{:S(2)}) copy-start(f32[1,96,3072]{2,1,0:T(8,128)} %param.23) | copy-start | bytes 3538948
  1.5 175.8 %collective-permute-start = (f32[3,256]{1,0:T(4,128)S(1)}, f32[3,256]{1,0:T(4,128)S(1)}, u32[]{:S(2)}, u32[]{:S(2)}) collective-permute-start(f32[3,256]{1,0:T(4,128)S(1)} %bitcast.182), channel_id=1, source_target_pairs={{0,32},{32,64},{64,96},{96,128},{128,160},{160,192},{192,224},{224... | collective-permute-start | bytes 9224 | tf_op jit(solution)/shard_map/ppermute | solution.py:26
  4.1 173.5 %collective-permute-start.1 = (f32[3,256]{1,0:T(4,128)S(1)}, f32[3,256]{1,0:T(4,128)S(1)}, u32[]{:S(2)}, u32[]{:S(2)}) collective-permute-start(f32[3,256]{1,0:T(4,128)S(1)} %bitcast.181), channel_id=1, source_target_pairs={{0,4},{1,5},{2,6},{3,7},{4,8},{5,9},{6,10},{7,11},{8,12},{9,13},{1... | collective-permute-start | bytes 9224 | tf_op jit(solution)/shard_map/ppermute | solution.py:26
  11.0 166.8 %collective-permute-start.2 = (f32[3,256]{1,0:T(4,128)S(1)}, f32[3,256]{1,0:T(4,128)S(1)}, u32[]{:S(2)}, u32[]{:S(2)}) collective-permute-start(f32[3,256]{1,0:T(4,128)S(1)} %bitcast.180), channel_id=1, source_target_pairs={{0,1},{1,2},{2,3},{3,4},{4,5},{5,6},{6,7},{7,8},{8,9},{9,10},{10,1... | collective-permute-start | bytes 9224 | tf_op jit(solution)/shard_map/ppermute | solution.py:26
  15.1 1.3 copy-start.8
  15.1 1.3 copy-start.4
  15.4 2.3 copy-start.9
  15.4 3.5 %copy-start.2 = (f32[1,96,384]{2,1,0:T(8,128)S(1)}, f32[1,96,384]{2,1,0:T(8,128)}, u32[]{:S(2)}) copy-start(f32[1,96,384]{2,1,0:T(8,128)} %param.24) | copy-start | bytes 442372
  15.6 157.1 %copy-start.5 = (f32[1,3,3,256]{3,0,2,1:T(1,128)S(1)}, f32[1,3,3,256]{3,0,2,1:T(1,128)}, u32[]{:S(2)}) copy-start(f32[1,3,3,256]{3,0,2,1:T(1,128)} %param.19) | copy-start | bytes 27652
  15.7 157.8 %copy-start.1 = (f32[384,384]{1,0:T(8,128)S(1)}, f32[384,384]{1,0:T(8,128)}, u32[]{:S(2)}) copy-start(f32[384,384]{1,0:T(8,128)} %param.25) | copy-start | bytes 1769476
  173.4 2.4 copy-start.3
  218.9 86.1 %copy-start.7 = (f32[1,3,3,256]{3,0,2,1:T(1,128)S(1)}, f32[1,3,3,256]{3,0,2,1:T(1,128)}, u32[]{:S(2)}) copy-start(f32[1,3,3,256]{3,0,2,1:T(1,128)} %param.17) | copy-start | bytes 27652
  218.9 86.7 %copy-start.6 = (f32[1,16,256]{2,1,0:T(8,128)S(1)}, f32[1,16,256]{2,1,0:T(8,128)}, u32[]{:S(2)}) copy-start(f32[1,16,256]{2,1,0:T(8,128)} %param.21) | copy-start | bytes 49156
  220.2 3.0 collective-permute-start.3
  221.9 2.5 collective-permute-start.5
  222.0 6.4 %collective-permute-start.4 = (f32[3,256]{1,0:T(4,128)S(1)}, f32[3,256]{1,0:T(4,128)S(1)}, u32[]{:S(2)}, u32[]{:S(2)}) collective-permute-start(f32[3,256]{1,0:T(4,128)S(1)} %reshape.732), channel_id=1, source_target_pairs={{0,28},{1,29},{2,30},{3,31},{4,0},{5,1},{6,2},{7,3},{8,4},{9,5},{1... | collective-permute-start | bytes 9224 | tf_op jit(solution)/shard_map/ppermute | solution.py:26
